TPU v7x, 512 devices: a whole 4x8x8 slice. The times are simulated.
512 devices in a mesh: row: 16 (over z, y_lo), col: 32 (over x, y_hi, core).
Axes of the slice: x: 4, y: 8 (y_hi: 4, y_lo: 2; y = y_hi * 2 + y_lo), z: 8, core: 2. Of those that a mesh axis runs over, the one named last changes fastest.
Arguments:
- green_blocks: bfloat16 [16, 32, 12, 2, 288, 288], P('row', 'col'), may hold values from -0.0625 to 0.0625
- slot_rows: int32 [16, 32, 12], P('row', 'col'), may hold values from 0 to 7, as said below
- slot_cols: int32 [16, 32, 12], P('row', 'col'), may hold values from 0 to 3
- slot_count: int32 [16, 32], P('row', 'col'), may hold values from 2 to 12, as said below
- cell_class: int32 [4, 32, 96], P(None, 'col'), may hold values from 0 to 15
- class_contrast: float32 [16, 2], replicated, may hold values from -0.6 to 0.6
- background: float32 [2, 32, 4, 32, 288], P(None, None, None, 'col'), may hold values from -6 to 6
Outputs:
- total_field: float32 [2, 32, 4, 32, 288], P(None, None, None, 'col')
Inputs may be any that keep to these rules, and one draw needn't show every extreme that they name: slot_rows[r, c, s] and slot_cols[r, c, s] name different block pairs within one device's slots, and every slot, used or not, names a block in the upper triangle: (slot_rows // 2) * 32 + 2 r + slot_rows % 2 is at most slot_cols * 32 + c. Slots from slot_count[r, c] on are not used. `slot_count`: some device holds exactly 12 stored blocks.
All inputs are finite; a program needn't handle non-finite values.
Results may differ from a plain program's by a relative error of at most 0.0033.
Values may be sent and summed in bfloat16 or wider, within the bound.
A program may use at most 64 MiB of HBM per device.

v0:
```python
import jax
import jax.numpy as jnp
from jax import lax
from jax.sharding import PartitionSpec as P

PRODUCTS = 3


def from_root(array, axis, root):
    mine = lax.axis_index(axis) == root
    return lax.psum(jnp.where(mine, array, jnp.zeros_like(array)), axis)


def complex_scale(field_now, contrast_re, contrast_im):
    real_part = field_now[0]
    imag_part = field_now[1]
    scaled = jnp.stack(
        [
            contrast_re * real_part - contrast_im * imag_part,
            contrast_re * imag_part + contrast_im * real_part,
        ]
    )
    return scaled.astype(jnp.bfloat16)


def combine(products):
    return jnp.stack([products[0, 0] - products[1, 1], products[0, 1] + products[1, 0]])


def local(green_blocks, slot_rows, slot_cols, slot_count, cell_class, class_contrast, background):
    row_index = lax.axis_index("row")
    col_index = lax.axis_index("col")
    stride = lax.axis_size("col")
    green_tiles = green_blocks[0, 0]
    slot_total = green_tiles.shape[0]
    entries = green_tiles.shape[-1]
    sources = background.shape[1]
    col_blocks = background.shape[2]
    row_blocks = 2 * col_blocks
    local_rows = slot_rows[0, 0]
    local_cols = slot_cols[0, 0]
    global_rows = local_rows // 2 * stride + 2 * row_index + local_rows % 2
    global_cols = local_cols * stride + col_index
    off_diagonal = (global_rows != global_cols).astype(jnp.float32)
    living = (jnp.arange(slot_total) < slot_count[0, 0]).astype(jnp.float32)
    row_pick = (local_rows[:, None] == jnp.arange(row_blocks)[None, :]).astype(
        jnp.float32
    ) * living[:, None]
    col_pick = (local_cols[:, None] == jnp.arange(col_blocks)[None, :]).astype(jnp.float32) * (
        living * off_diagonal
    )[:, None]
    classes = class_contrast.shape[0]
    lookup = (cell_class[:, 0, :, None] == jnp.arange(classes)[None, None, :]).astype(jnp.float32)
    values = jnp.einsum("bte,ec->btc", lookup, class_contrast, precision=lax.Precision.HIGHEST)
    contrast_re = jnp.tile(values[:, :, 0], (1, 3))
    contrast_im = jnp.tile(values[:, :, 1], (1, 3))
    start_field = background[:, :, :, 0, :]
    field_now = start_field
    current = complex_scale(field_now, contrast_re, contrast_im)
    for step_index in range(PRODUCTS):
        final_step = step_index + 1 == PRODUCTS
        halves = [from_root(current, "col", 2 * row_index + parity) for parity in range(2)]
        row_current = jnp.stack(halves, axis=3).reshape(2, sources, row_blocks, entries)
        direct_in = jnp.take(current, local_cols, axis=2)
        mirror_in = jnp.take(row_current, local_rows, axis=2)
        direct_terms = combine(
            jnp.einsum(
                "sqoi,pksi->qpkso", green_tiles, direct_in, preferred_element_type=jnp.float32
            )
        )
        mirror_terms = combine(
            jnp.einsum(
                "sqoi,pkso->qpksi", green_tiles, mirror_in, preferred_element_type=jnp.float32
            )
        )
        direct_part = jnp.einsum(
            "pkse,sb->pkbe", direct_terms, row_pick, precision=lax.Precision.HIGHEST
        )
        mirror_part = jnp.einsum(
            "pkse,sb->pkbe", mirror_terms, col_pick, precision=lax.Precision.HIGHEST
        )
        row_total = lax.psum(direct_part, "col")
        owned_part = lax.dynamic_index_in_dim(
            row_total.reshape(2, sources, col_blocks, 2, entries),
            col_index % 2,
            axis=3,
            keepdims=False,
        )
        direct_here = from_root(owned_part, "row", col_index // 2)
        column_total = lax.psum(mirror_part, "row")
        field_now = start_field + column_total + direct_here
        if not final_step:
            current = complex_scale(field_now, contrast_re, contrast_im)
    return field_now[:, :, :, None, :]


def solution(mesh):
    in_specs = (
        P("row", "col", None, None, None, None),
        P("row", "col", None),
        P("row", "col", None),
        P("row", "col"),
        P(None, "col", None),
        P(),
        P(None, None, None, "col", None),
    )
    out_specs = P(None, None, None, "col", None)
    return jax.shard_map(local, mesh=mesh, in_specs=in_specs, out_specs=out_specs, check_vma=False)
```

profile of v0, /device:TPU:1, one launch (start us, length us, event | category | flops | bytes accessed | tf_op | source)
XLA Modules:
  0.0 2174.7 jit_solution(12541447128961993889)
XLA Ops:
  6.6 0.7 copy-done
  7.2 0.8 fusion.106
  8.0 0.1 tile.20
  8.1 0.1 tile.23
  8.2 1.3 fusion.152
  9.5 0.1 subtract_convert_fusion.2
  9.6 1.0 select_bitcast_fusion.8
  10.8 0.7 gather_fusion.1
  11.5 4.6 fusion.15
  16.1 0.1 fusion.72
  16.2 0.1 fusion.74
  16.9 0.1 pad_maximum_fusion.1
  17.0 1.5 fusion.42
  18.6 0.2 copy.42
  18.8 1.5 copy.43
  20.4 272.8 %all-reduce.32.cloned.1.call-done = (bf16[2,32,4,1,288]{4,2,1,0,3:T(4,128)(2,1)}, bf16[2,32,4,1,288]{4,2,1,0,3:T(4,128)(2,1)}) async-done(((bf16[2,32,4,1,288]{4,2,1,0,3:T(4,128)(2,1)}, bf16[2,32,4,1,288]{4,2,1,0,3:T(4,128)(2,1)}), (bf16[2,32,4,1,288]{4,2,1,0,3:T(4,128)(2,1)}, bf16[2,32,4,1,288]{4,2,1,0,3:T(4,128)(2,1)})) %all-reduce.32.cloned.1.call-update) | async-done | bytes 294928 | tf_op jit(solution)/shard_map/psum | solution.py:11
  293.2 1.3 pad_maximum_fusion.6
  294.5 0.7 gather_fusion
  295.2 3.8 fusion.12
  299.2 0.1 pad_maximum_fusion
  299.3 2.3 fusion.51
  301.6 282.1 %all-reduce.16.cloned.1.call-done = f32[2,32,4,2,288]{4,2,1,0,3:T(4,128)} async-done(((f32[2,32,4,2,288]{4,2,1,0,3:T(4,128)}), f32[2,32,4,2,288]{4,2,1,0,3:T(4,128)}) %all-reduce.16.cloned.1.call-update) | async-done | bytes 589840 | tf_op jit(solution)/shard_map/psum | solution.py:82
  583.8 1.8 select_bitcast_fusion.2
  585.7 135.6 %all-reduce.26.cloned.1.call-done = (f32[2,32,4,288]{3,2,1,0:T(4,128)}, f32[2,32,4,288]{3,2,1,0:T(4,128)}) async-done(((f32[2,32,4,288]{3,2,1,0:T(4,128)}, f32[2,32,4,288]{3,2,1,0:T(4,128)}), (f32[2,32,4,288]{3,2,1,0:T(4,128)}, f32[2,32,4,288]{3,2,1,0:T(4,128)})) %all-reduce.26.cloned.1.call-update) | async-done | bytes 589840 | tf_op jit(solution)/shard_map/psum | solution.py:11
  721.3 1.3 fusion.96
  722.6 0.1 subtract_convert_fusion.1
  722.7 1.0 select_bitcast_fusion.6
  723.8 0.7 gather_fusion.3
  724.4 4.6 fusion.21
  729.2 0.2 all-reduce.18.cloned.1.call-start
  729.5 0.1 pad_maximum_fusion.3
  729.6 1.5 fusion.45
  731.1 0.2 copy.52
  731.3 1.5 copy.53
  732.8 282.8 %all-reduce.30.cloned.1.call-done = (bf16[2,32,4,1,288]{4,2,1,0,3:T(4,128)(2,1)}, bf16[2,32,4,1,288]{4,2,1,0,3:T(4,128)(2,1)}) async-done(((bf16[2,32,4,1,288]{4,2,1,0,3:T(4,128)(2,1)}, bf16[2,32,4,1,288]{4,2,1,0,3:T(4,128)(2,1)}), (bf16[2,32,4,1,288]{4,2,1,0,3:T(4,128)(2,1)}, bf16[2,32,4,1,288]{4,2,1,0,3:T(4,128)(2,1)})) %all-reduce.30.cloned.1.call-update) | async-done | bytes 294928 | tf_op jit(solution)/shard_map/psum | solution.py:11
  1015.6 1.3 pad_maximum_fusion.7
  1017.0 0.7 gather_fusion.2
  1017.7 3.8 fusion.18
  1021.6 0.1 pad_maximum_fusion.2
  1021.7 2.3 fusion.54
  1024.1 281.7 %all-reduce.18.cloned.1.call-done = f32[2,32,4,2,288]{4,2,1,0,3:T(4,128)} async-done(((f32[2,32,4,2,288]{4,2,1,0,3:T(4,128)}), f32[2,32,4,2,288]{4,2,1,0,3:T(4,128)}) %all-reduce.18.cloned.1.call-update) | async-done | bytes 589840 | tf_op jit(solution)/shard_map/psum | solution.py:82
  1305.8 1.8 select_bitcast_fusion.1
  1307.7 135.6 %all-reduce.24.cloned.1.call-done = (f32[2,32,4,288]{3,2,1,0:T(4,128)}, f32[2,32,4,288]{3,2,1,0:T(4,128)}) async-done(((f32[2,32,4,288]{3,2,1,0:T(4,128)}, f32[2,32,4,288]{3,2,1,0:T(4,128)}), (f32[2,32,4,288]{3,2,1,0:T(4,128)}, f32[2,32,4,288]{3,2,1,0:T(4,128)})) %all-reduce.24.cloned.1.call-update) | async-done | bytes 589840 | tf_op jit(solution)/shard_map/psum | solution.py:11
  1443.4 1.3 fusion.97
  1444.7 0.1 subtract_convert_fusion
  1444.8 1.0 select_bitcast_fusion.4
  1445.8 0.7 gather_fusion.5
  1446.5 4.6 fusion.27
  1451.4 0.1 pad_maximum_fusion.5
  1451.5 1.5 fusion.48
  1453.0 0.2 copy.62
  1453.2 1.5 copy.63
  1454.7 0.3 all-reduce.22.cloned.1.call-start
  1454.9 282.8 %all-reduce.28.cloned.1.call-done = (bf16[2,32,4,1,288]{4,2,1,0,3:T(4,128)(2,1)}, bf16[2,32,4,1,288]{4,2,1,0,3:T(4,128)(2,1)}) async-done(((bf16[2,32,4,1,288]{4,2,1,0,3:T(4,128)(2,1)}, bf16[2,32,4,1,288]{4,2,1,0,3:T(4,128)(2,1)}), (bf16[2,32,4,1,288]{4,2,1,0,3:T(4,128)(2,1)}, bf16[2,32,4,1,288]{4,2,1,0,3:T(4,128)(2,1)})) %all-reduce.28.cloned.1.call-update) | async-done | bytes 294928 | tf_op jit(solution)/shard_map/psum | solution.py:11
  1737.7 1.3 pad_maximum_fusion.8
  1739.1 0.7 gather_fusion.4
  1739.8 3.8 fusion.24
  1743.7 0.1 pad_maximum_fusion.4
  1743.8 2.3 fusion.57
  1746.1 282.2 %all-reduce.20.cloned.1.call-done = f32[2,32,4,2,288]{4,2,1,0,3:T(4,128)} async-done(((f32[2,32,4,2,288]{4,2,1,0,3:T(4,128)}), f32[2,32,4,2,288]{4,2,1,0,3:T(4,128)}) %all-reduce.20.cloned.1.call-update) | async-done | bytes 589840 | tf_op jit(solution)/shard_map/psum | solution.py:82
  2028.3 1.8 select_bitcast_fusion
  2030.2 135.5 %all-reduce.22.cloned.1.call-done = (f32[2,32,4,288]{3,2,1,0:T(4,128)}, f32[2,32,4,288]{3,2,1,0:T(4,128)}) async-done(((f32[2,32,4,288]{3,2,1,0:T(4,128)}, f32[2,32,4,288]{3,2,1,0:T(4,128)}), (f32[2,32,4,288]{3,2,1,0:T(4,128)}, f32[2,32,4,288]{3,2,1,0:T(4,128)})) %all-reduce.22.cloned.1.call-update) | async-done | bytes 589840 | tf_op jit(solution)/shard_map/psum | solution.py:11
  2165.7 1.3 fusion.99
  2167.0 1.1 copy.64
  (48 shorter events, 1.4 us)
Async XLA Ops:
  6.5 0.7 copy-start
  6.5 4.2 copy-start.3
  6.5 4.2 copy-start.2
  6.5 286.6 %all-reduce.32.cloned.1.call-start = ((), (), s32[]{:S(2)}) async-start(), calls=%async_computation.8 | async-start | bytes 786432 | tf_op jit(solution)/shard_map/psum | solution.py:11
  10.7 573.1 %all-reduce.16.cloned.1.call-start = ((), (), s32[]{:S(2)}) async-start(), calls=%async_computation | async-start | bytes 1572864 | tf_op jit(solution)/shard_map/psum | solution.py:82
  20.2 701.0 %all-reduce.26.cloned.1.call-start = ((), (), s32[]{:S(2)}) async-start(), calls=%async_computation.5 | async-start | bytes 1572864 | tf_op jit(solution)/shard_map/psum | solution.py:11
  299.3 422.0 %copy-start.1 = (f32[2,32,4,1,288]{4,3,2,1,0:T(1,128)S(1)}, f32[2,32,4,1,288]{4,3,2,1,0:T(1,128)}, u32[]{:S(2)}) copy-start(f32[2,32,4,1,288]{4,3,2,1,0:T(1,128)} %param.17) | copy-start | bytes 884740
  585.6 430.0 %all-reduce.30.cloned.1.call-start = ((), (), s32[]{:S(2)}) async-start(), calls=%async_computation.7 | async-start | bytes 786432 | tf_op jit(solution)/shard_map/psum | solution.py:11
  729.2 576.6 %all-reduce.18.cloned.1.call-start = ((), (), s32[]{:S(2)}) async-start(), calls=%async_computation.1 | async-start | bytes 1572864 | tf_op jit(solution)/shard_map/psum | solution.py:82
  732.8 710.6 %all-reduce.24.cloned.1.call-start = ((), (), s32[]{:S(2)}) async-start(), calls=%async_computation.4 | async-start | bytes 1572864 | tf_op jit(solution)/shard_map/psum | solution.py:11
  1307.7 430.0 %all-reduce.28.cloned.1.call-start = ((), (), s32[]{:S(2)}) async-start(), calls=%async_computation.6 | async-start | bytes 786432 | tf_op jit(solution)/shard_map/psum | solution.py:11
  1451.3 577.0 %all-reduce.20.cloned.1.call-start = ((), (), s32[]{:S(2)}) async-start(), calls=%async_computation.2 | async-start | bytes 1572864 | tf_op jit(solution)/shard_map/psum | solution.py:82
  1454.7 711.0 %all-reduce.22.cloned.1.call-start = ((), (), s32[]{:S(2)}) async-start(), calls=%async_computation.3 | async-start | bytes 1572864 | tf_op jit(solution)/shard_map/psum | solution.py:11
Sparse Core Ops, SparseCore 0:
  10.8 282.2 all-reduce.31
  296.3 287.4 all-reduce.15
  586.7 134.5 all-reduce.25
  729.4 286.2 all-reduce.29
  1018.4 287.4 all-reduce.17
  1308.9 134.4 all-reduce.23
  1451.5 286.1 all-reduce.27
  1740.8 287.4 all-reduce.19
  2031.3 134.3 all-reduce.21
where the time goes:
time: 2180 us; the launch traced here: 2170 us
  waiting for transfers between devices  2090 us (96%)
  matrix products  37.7 us (2%)
    psum x6, waiting for transfers between devices, from_root(): return lax.psum(jnp.where(mine, array, jnp.zeros_like(array)), axis)  1250 us
    psum x3, waiting for transfers between devices, local(): row_total = lax.psum(direct_part, 'col')  846 us
  transfers between devices with their start and end apart: 9, of which 9 were waited for; matrix products, arithmetic and copies ran while one was open for 2% of the time, Pallas kernels for 0%

commit v1 on v0

v1 whole, which is shorter than its diff:
```python
import functools

import jax
import jax.numpy as jnp
from jax import lax
from jax.experimental import pallas as pl
from jax.experimental.pallas import tpu as pltpu
from jax.sharding import PartitionSpec as P

PRODUCTS = 3
SHARDS = 12
GROUPS = 4
MESH = pl.DeviceIdType.MESH
F32 = jnp.float32
BF16 = jnp.bfloat16
NT = (((1,), (1,)), ((), ()))
NN = (((1,), (0,)), ((), ()))


def pack(field):
    rows = field.reshape(2, GROUPS, 8, 4, 288).transpose(1, 0, 2, 3, 4).reshape(GROUPS, 16, 4, 288)
    main = rows[..., :256].reshape(GROUPS, 16, 1024)
    tail = rows[..., 256:].reshape(GROUPS, 16, 128)
    lanes = jnp.concatenate([main, tail], axis=-1).reshape(GROUPS, 16, 3, 384)
    return lanes.transpose(0, 2, 1, 3).reshape(SHARDS, 16, 384)


def unpack(shards):
    lanes = shards.reshape(GROUPS, 3, 16, 384).transpose(0, 2, 1, 3).reshape(GROUPS, 16, 1152)
    main = lanes[..., :1024].reshape(GROUPS, 16, 4, 256)
    tail = lanes[..., 1024:].reshape(GROUPS, 16, 4, 32)
    rows = jnp.concatenate([main, tail], axis=-1).reshape(GROUPS, 2, 8, 4, 288)
    return rows.transpose(1, 0, 2, 3, 4).reshape(2, 32, 4, 288)


def kernel(
    n_rows,
    rows_ref,
    cols_ref,
    row_pick,
    col_pick,
    g_hbm,
    first_ref,
    back_ref,
    scale_ref,
    out_ref,
    g,
    own,
    across,
    left_own,
    left_across,
    terms,
    half,
    half_in,
    direct,
    mirror,
    arrived,
    now,
    g_sem,
    own_sem,
    across_sem,
    swap_sem,
    half_sem,
    arrived_sem,
    out_sem,
    send_first,
    send_swap,
    send_half,
    send_direct,
    send_mirror,
    send_now,
):
    slots = g.shape[0]
    r = lax.axis_index("row")
    c = lax.axis_index("col")
    s, k = c // 2, c % 2
    shard = (r - s + n_rows) % n_rows
    diagonal = r == s
    reducer = shard < SHARDS
    other = (r, 2 * s + 1 - k)

    loads = pltpu.make_async_copy(g_hbm.at[0, 0], g, g_sem)
    loads.start()

    barrier = pltpu.get_barrier_semaphore()

    def greet(row, col):
        pl.semaphore_signal(barrier, inc=1, device_id=(row, col), device_id_type=MESH)

    greet(*other)

    def greet_all(d, _):
        @pl.when(d > 0)
        def _():
            greet((r + d) % n_rows, c)

        @pl.when(jnp.logical_and(d > 0, (s + d) % n_rows != r))
        def _():
            greet(s, 2 * ((s + d) % n_rows) + k)

        @pl.when(jnp.logical_not(diagonal))
        def _():
            greet((r + d) % n_rows, 2 * r + k)

        return 0

    lax.fori_loop(0, n_rows, greet_all, 0)

    def send(src, dst, send_sem, recv_sem, row, col):
        pltpu.make_async_remote_copy(
            src_ref=src,
            dst_ref=dst,
            send_sem=send_sem,
            recv_sem=recv_sem,
            device_id=(row, col),
            device_id_type=MESH,
        ).start()

    def take(ref, sem):
        pltpu.make_async_copy(ref, ref, sem).wait()

    def unfold(packed, lefts):
        def group(i, _):
            at = pl.ds(pl.multiple_of(16 * i, 16), 16)

            def put(q, lane, value):
                turned = jnp.concatenate([-value[8:], value[:8]], axis=0)
                lefts[q, 0, at, lane : lane + 128] = value.astype(BF16)
                lefts[q, 1, at, lane : lane + 128] = turned.astype(BF16)

            for tile in range(8):
                value = packed[3 * i + tile // 3, :, 128 * (tile % 3) : 128 * (tile % 3) + 128]
                put(tile // 2, 128 * (tile % 2), value.astype(F32))
            tail = packed[3 * i + 2, :, 256:384].astype(F32)
            put(0, 256, tail)
            for q in range(1, 4):
                put(q, 256, pltpu.roll(tail, 128 - 32 * q, 1))
            return 0

        lax.fori_loop(0, GROUPS, group, 0)

    def products(lefts, picks, dims):
        def one(slot, _):
            at = picks[slot]
            re = lefts[at, 0, :, :288]
            im = lefts[at, 1, :, :288]
            terms[slot, :, :288] = lax.dot_general(
                re, g[slot, 0], dims, preferred_element_type=F32
            ) + lax.dot_general(im, g[slot, 1], dims, preferred_element_type=F32)
            return 0

        lax.fori_loop(0, slots, one, 0)

    def gather_terms(pick, first, step, out):
        def group(i, _):
            at = pl.ds(pl.multiple_of(16 * i, 16), 16)
            tail = None
            for q in range(4):
                total = None
                for slot in range(slots):
                    value = terms[slot, at, :] * pick[(first + step * q) * slots + slot]
                    total = value if total is None else total + value
                for part in range(2):
                    tile = 2 * q + part
                    out[3 * i + tile // 3, :, 128 * (tile % 3) : 128 * (tile % 3) + 128] = total[
                        :, 128 * part : 128 * part + 128
                    ].astype(out.dtype)
                last = total[:, 256:384]
                last = pltpu.roll(last, 32 * q, 1) if q else last
                tail = last if tail is None else tail + last
            out[3 * i + 2, :, 256:384] = tail.astype(out.dtype)
            return 0

        lax.fori_loop(0, GROUPS, group, 0)

    terms[:, :, 256:384] = jnp.zeros((slots, 64, 128), F32)
    unfold(first_ref, left_own)

    @pl.when(jnp.logical_not(diagonal))
    def _():
        pl.semaphore_wait(barrier, 3 * n_rows - 2)
        send(first_ref, across.at[0, k], send_first, across_sem.at[0], s, 2 * r + k)

    @pl.when(diagonal)
    def _():
        pl.semaphore_wait(barrier, 2 * n_rows - 1)
        pltpu.make_async_copy(first_ref, across.at[0, k], across_sem.at[0]).start()

    loads.wait()

    def update(step, final):
        products(left_own, cols_ref, NT)
        gather_terms(row_pick, 1 - k, 2, half.at[step, 1])
        send(half.at[step, 1], half_in.at[step], send_half.at[step], half_sem.at[step], *other)
        gather_terms(row_pick, k, 2, half.at[step, 0])

        take(across.at[step, k], across_sem.at[step])
        send(across.at[step, k], across.at[step, k], send_swap.at[step], swap_sem.at[step], *other)

        take(half_in.at[step], half_sem.at[step])

        def send_one(t, _):
            direct[step, t] = (half[step, 0, t] + half_in[step, t]).astype(BF16)
            row = (r + t) % n_rows
            mine = jnp.logical_and(diagonal, t == 0)
            dst = arrived.at[step, s]

            @pl.when(mine)
            def _():
                pltpu.make_async_copy(direct.at[step, t], dst, arrived_sem.at[step]).start()

            @pl.when(jnp.logical_not(mine))
            def _():
                send(direct.at[step, t], dst, send_direct.at[step], arrived_sem.at[step], row, 2 * r + k)

            return 0

        lax.fori_loop(0, SHARDS, send_one, 0)

        unfold(across.at[step, k], left_across.at[k])
        take(across.at[step, 1 - k], swap_sem.at[step])
        unfold(across.at[step, 1 - k], left_across.at[1 - k])
        products_across()
        gather_terms(col_pick, 0, 1, mirror.at[step])

        def send_mine(t, _):
            row = (s + t) % n_rows
            mine = row == r
            dst = arrived.at[step, n_rows + r]

            @pl.when(mine)
            def _():
                pltpu.make_async_copy(mirror.at[step, t], dst, arrived_sem.at[step]).start()

            @pl.when(jnp.logical_not(mine))
            def _():
                send(mirror.at[step, t], dst, send_mirror.at[step], arrived_sem.at[step], row, c)

            return 0

        lax.fori_loop(0, SHARDS, send_mine, 0)

        @pl.when(reducer)
        def _():
            take(arrived.at[step], arrived_sem.at[step])

            def add(j, total):
                return total + arrived[step, j].astype(F32)

            field = lax.fori_loop(0, 2 * n_rows, add, back_ref[shard], unroll=4)
            if final:
                out_ref[shard] = field
            else:
                re, im = field[:8], field[8:]
                scale_re, scale_im = scale_ref[0, shard % 3], scale_ref[1, shard % 3]
                now[step, :8] = (scale_re * re - scale_im * im).astype(BF16)
                now[step, 8:] = (scale_re * im + scale_im * re).astype(BF16)

        if final:
            return

        @pl.when(reducer)
        def _():
            src = now.at[step]
            line = own.at[step, shard]
            plane = across.at[step + 1, k, shard]
            pltpu.make_async_copy(src, line, own_sem.at[step]).start()

            def spread(d, _):
                @pl.when(jnp.logical_or(d > 0, r != s))
                def _():
                    send(src, plane, send_now.at[step], across_sem.at[step + 1], s, 2 * ((s + d) % n_rows) + k)

                @pl.when(jnp.logical_and(d == 0, r == s))
                def _():
                    pltpu.make_async_copy(src, plane, across_sem.at[step + 1]).start()

                @pl.when(d > 0)
                def _():
                    send(src, line, send_now.at[step], own_sem.at[step], (r + d) % n_rows, c)

                return 0

            lax.fori_loop(0, n_rows, spread, 0)

        take(own.at[step], own_sem.at[step])
        unfold(own.at[step], left_own)

    def products_across():
        def one(slot, _):
            at = rows_ref[slot]
            re = left_across[at % 2, at // 2, 0, :, :288]
            im = left_across[at % 2, at // 2, 1, :, :288]
            terms[slot, :, :288] = lax.dot_general(
                re, g[slot, 0], NN, preferred_element_type=F32
            ) + lax.dot_general(im, g[slot, 1], NN, preferred_element_type=F32)
            return 0

        lax.fori_loop(0, slots, one, 0)

    def early(step, _):
        update(step, False)
        return 0

    lax.fori_loop(0, PRODUCTS - 1, early, 0)
    update(PRODUCTS - 1, True)

    @pl.when(reducer)
    def _():
        def spread(d, _):
            send(out_ref.at[shard], out_ref.at[shard], send_now.at[PRODUCTS - 1], out_sem, (r + d) % n_rows, c)
            return 0

        lax.fori_loop(1, n_rows, spread, 0)
        take(out_ref.at[pl.ds(0, SHARDS - 1)], out_sem)
        take(half.at[0, 0], send_now.at[PRODUCTS - 1])
        take(half.at[0, 0, pl.ds(0, n_rows - 1 - SHARDS)], send_now.at[PRODUCTS - 1])

    @pl.when(jnp.logical_not(reducer))
    def _():
        take(out_ref, out_sem)

    @pl.when(jnp.logical_not(diagonal))
    def _():
        take(first_ref, send_first)

    def finish(step, _):
        take(across.at[step, 0], send_swap.at[step])
        take(half_in.at[step], send_half.at[step])

        @pl.when(diagonal)
        def _():
            take(direct.at[step, pl.ds(0, SHARDS - 1)], send_direct.at[step])

        @pl.when(jnp.logical_not(diagonal))
        def _():
            take(direct.at[step], send_direct.at[step])

        @pl.when(reducer)
        def _():
            take(mirror.at[step, pl.ds(0, SHARDS - 1)], send_mirror.at[step])

            @pl.when(step < PRODUCTS - 1)
            def _():
                @pl.when(diagonal)
                def _():
                    take(arrived.at[step, pl.ds(0, 2 * n_rows - 2)], send_now.at[step])

                @pl.when(jnp.logical_not(diagonal))
                def _():
                    take(arrived.at[step, pl.ds(0, 2 * n_rows - 1)], send_now.at[step])

        @pl.when(jnp.logical_not(reducer))
        def _():
            take(mirror.at[step], send_mirror.at[step])

        return 0

    lax.fori_loop(0, PRODUCTS, finish, 0)


def local(n_rows, green_blocks, slot_rows, slot_cols, slot_count, cell_class, class_contrast, background):
    row_index = lax.axis_index("row")
    col_index = lax.axis_index("col")
    stride = lax.axis_size("col")
    slots = green_blocks.shape[2]
    local_rows = slot_rows[0, 0]
    local_cols = slot_cols[0, 0]
    global_rows = local_rows // 2 * stride + 2 * row_index + local_rows % 2
    global_cols = local_cols * stride + col_index
    living = jnp.arange(slots) < slot_count[0, 0]
    row_pick = jnp.where(living & (local_rows == jnp.arange(8)[:, None]), 1.0, 0.0).reshape(-1)
    col_pick = jnp.where(
        living & (global_rows != global_cols) & (local_cols == jnp.arange(4)[:, None]), 1.0, 0.0
    ).reshape(-1)

    classes = class_contrast.shape[0]
    at = cell_class[:, 0, None, :] == jnp.arange(classes)[None, :, None]
    scale = jnp.stack(
        [jnp.sum(jnp.where(at, class_contrast[None, :, part, None], 0.0), axis=1) for part in range(2)]
    )
    scale = jnp.tile(scale, (1, 1, 3))
    lanes = jnp.concatenate(
        [scale[..., :256].reshape(2, 1024), scale[..., 256:].reshape(2, 128)], axis=-1
    ).reshape(2, 3, 1, 384)
    scale = jnp.broadcast_to(lanes, (2, 3, 8, 384))

    back = pack(background[:, :, :, 0, :])
    pairs = back.reshape(GROUPS, 3, 2, 8, 384)
    re, im = pairs[:, :, 0], pairs[:, :, 1]
    first = (
        jnp.stack([scale[0] * re - scale[1] * im, scale[0] * im + scale[1] * re], axis=2)
        .astype(BF16)
        .reshape(SHARDS, 16, 384)
    )

    vmem = pl.BlockSpec(memory_space=pltpu.VMEM)
    smem = pl.BlockSpec(memory_space=pltpu.SMEM)
    packed = (SHARDS, 16, 384)
    steps = (PRODUCTS,)
    dma = pltpu.SemaphoreType.DMA
    field = pl.pallas_call(
        functools.partial(kernel, n_rows),
        out_shape=jax.ShapeDtypeStruct(packed, F32),
        in_specs=[smem] * 4 + [pl.BlockSpec(memory_space=pl.ANY)] + [vmem] * 3,
        out_specs=vmem,
        scratch_shapes=[
            pltpu.VMEM(green_blocks.shape[2:], BF16),
            pltpu.VMEM((PRODUCTS - 1,) + packed, BF16),
            pltpu.VMEM((PRODUCTS, 2) + packed, BF16),
            pltpu.VMEM((4, 2, 64, 384), BF16),
            pltpu.VMEM((2, 4, 2, 64, 384), BF16),
            pltpu.VMEM((slots, 64, 384), F32),
            pltpu.VMEM((PRODUCTS, 2) + packed, F32),
            pltpu.VMEM(steps + packed, F32),
            pltpu.VMEM(steps + packed, BF16),
            pltpu.VMEM(steps + packed, BF16),
            pltpu.VMEM((PRODUCTS, 2 * n_rows, 16, 384), BF16),
            pltpu.VMEM((PRODUCTS, 16, 384), BF16),
            dma(()),
            dma((PRODUCTS - 1,)),
            dma(steps),
            dma(steps),
            dma(steps),
            dma(steps),
            dma(()),
            dma(()),
            dma(steps),
            dma(steps),
            dma(steps),
            dma(steps),
            dma(steps),
        ],
        compiler_params=pltpu.CompilerParams(
            collective_id=0, has_side_effects=True, vmem_limit_bytes=48 * 2**20
        ),
    )(local_rows, local_cols, row_pick, col_pick, green_blocks, first, back, scale)
    return unpack(field)[:, :, :, None, :]


def solution(mesh):
    in_specs = (
        P("row", "col", None, None, None, None),
        P("row", "col", None),
        P("row", "col", None),
        P("row", "col"),
        P(None, "col", None),
        P(),
        P(None, None, None, "col", None),
    )
    out_specs = P(None, None, None, "col", None)
    return jax.shard_map(
        functools.partial(local, mesh.shape["row"]),
        mesh=mesh,
        in_specs=in_specs,
        out_specs=out_specs,
        check_vma=False,
    )
```

time: 2180 us -> 137 us (0.06)
  waiting for transfers between devices: 2090 us -> 0 us
  Pallas kernels: 0 us -> 128 us
  matrix products: 37.7 us -> 0 us
    psum x9 -> x0, waiting for transfers between devices: 2090 us -> none  [the longest x6 1250 us: from_root(): return lax.psum(jnp.where(mine, array, jnp.zeros_like(array)), axis)]
    pallas_call x0 -> x1, Pallas kernels: none -> 128 us  [local(): pl.pallas_call(functools.partial(kernel, n_rows), out_shape=jax.ShapeDtyp...]
    dot_general x13 -> x0, matrix products: 37.7 us -> none  [the longest x3 13.9 us: local(): jnp.einsum('sqoi,pksi->qpkso', green_tiles, direct_in, preferred_element_...]
  transfers between devices with their start and end apart: 9 -> 0, of which waited for: 9 -> 0; matrix products, arithmetic and copies ran while one was open for 2% -> 0% of each run, Pallas kernels for 0% -> 0%
where the time goes in v1:
time: 137 us
  Pallas kernels  128 us (93%)
  local copies, waits for them, and re-layouts  6.92 us (5%)
    pallas_call x1, Pallas kernels, local(): pl.pallas_call(functools.partial(kernel, n_rows), out_shape=jax.ShapeDtyp...  128 us

profile of v1, /device:TPU:1, one launch (start us, length us, event | category | flops | bytes accessed | tf_op | source)
XLA Modules:
  0.0 136.7 jit_solution(13171108301944854064)
XLA Ops:
  0.0 0.0 copy-start.1
  0.0 0.0 copy-start.2
  0.0 0.8 slice_bitcast_fusion.2
  0.8 0.8 select_reduce_fusion.1
  1.6 0.1 tile.10
  1.7 0.1 reshape.137
  1.8 1.0 copy_bitcast_fusion.2
  2.9 0.1 copy.25
  3.0 0.1 reshape.140
  3.1 0.1 reshape.141
  3.3 0.1 fusion.5
  4.1 0.0 copy-done.1
  4.1 0.0 copy-done.2
  4.2 0.1 select_n.44.row_pick
  4.3 0.1 select_n.48.col_pick
  4.4 0.0 copy-start
  4.4 2.5 %copy-done = bf16[1,1,12,2,288,288]{5,4,3,2,1,0:T(8,128)(2,1)S(1)} copy-done((bf16[1,1,12,2,288,288]{5,4,3,2,1,0:T(8,128)(2,1)S(1)}, bf16[1,1,12,2,288,288]{5,4,3,2,1,0:T(8,128)(2,1)}, u32[]{:S(2)}) %copy-start) | copy-done | bytes 3981336
  6.9 127.9 %shard_map.73 = f32[12,16,384]{2,1,0:T(8,128)S(1)} custom-call(s32[12]{0:T(128)S(1)} %bitcast.44, s32[12]{0:T(128)S(1)} %bitcast.46, f32[96]{0:T(128)S(1)} %select_n.44.row_pick, f32[48]{0:T(128)S(1)} %select_n.48.col_pick, bf16[1,1,12,2,288,288]{5,4,3,2,1,0:T(8,128)(2,1)S(1)} %copy-done, bf16[12,16,384]{2,1,0:T(8,128)(2,1)S(1)} %bitcast.42, ...), custom_call_target="tpu_custom_call" | custom-call | tf_op jit(solution)/shard_map/pallas_call | solution.py:402
  134.8 0.2 copy.46
  135.0 0.2 reshape.144
  135.2 0.1 concatenate.16
  135.3 0.1 concatenate.17
  135.4 0.1 maximum_bitcast_fusion
  135.6 1.2 copy.31
  (25 shorter events, 0.4 us)
Async XLA Ops:
  0.0 4.1 %copy-start.1 = (s32[1,1,12]{2,1,0:T(1,128)S(1)}, s32[1,1,12]{2,1,0:T(1,128)}, u32[]{:S(2)}) copy-start(s32[1,1,12]{2,1,0:T(1,128)} %param.8) | copy-start | bytes 148
  0.0 4.1 %copy-start.2 = (s32[1,1,12]{2,1,0:T(1,128)S(1)}, s32[1,1,12]{2,1,0:T(1,128)}, u32[]{:S(2)}) copy-start(s32[1,1,12]{2,1,0:T(1,128)} %param.9) | copy-start | bytes 148
  4.4 2.5 %copy-start = (bf16[1,1,12,2,288,288]{5,4,3,2,1,0:T(8,128)(2,1)S(1)}, bf16[1,1,12,2,288,288]{5,4,3,2,1,0:T(8,128)(2,1)}, u32[]{:S(2)}) copy-start(bf16[1,1,12,2,288,288]{5,4,3,2,1,0:T(8,128)(2,1)} %g_hbm.1) | copy-start | bytes 11943940

commit v2 on v1

--- a/solution.py
+++ b/solution.py
@@ -9,6 +9,7 @@
 
 PRODUCTS = 3
 SHARDS = 12
+TURN = 4
 GROUPS = 4
 MESH = pl.DeviceIdType.MESH
 F32 = jnp.float32
@@ -56,6 +57,9 @@
     mirror,
     arrived,
     now,
+    last,
+    give,
+    given,
     g_sem,
     own_sem,
     across_sem,
@@ -69,15 +73,31 @@
     send_direct,
     send_mirror,
     send_now,
+    given_sem,
+    send_given,
 ):
     slots = g.shape[0]
     r = lax.axis_index("row")
     c = lax.axis_index("col")
     s, k = c // 2, c % 2
-    shard = (r - s + n_rows) % n_rows
+    side = n_rows // 4
     diagonal = r == s
-    reducer = shard < SHARDS
     other = (r, 2 * s + 1 - k)
+
+    def turn(row):
+        return (row // 2) % TURN
+
+    def place(t):
+        return 4 * (t // 3) + t % 3 + (t % 3) // 2 * (t // 3 % 2)
+
+    def seat(h, row):
+        return (h // side + turn(row)) % 4 * side + h % side
+
+    hub = (s // side + 4 - turn(r)) % 4 * side + s % side
+    reducer = jnp.logical_or(r % 4 < 2, r % 4 == 2 + r // 4 % 2)
+    shard = 3 * (r // 4) + jnp.minimum(r % 4, 2)
+    in_line = jnp.logical_and(reducer, hub == s)
+    in_plane = jnp.logical_and(reducer, hub == r)
 
     loads = pltpu.make_async_copy(g_hbm.at[0, 0], g, g_sem)
     loads.start()
@@ -89,22 +109,48 @@
 
     greet(*other)
 
-    def greet_all(d, _):
-        @pl.when(d > 0)
-        def _():
-            greet((r + d) % n_rows, c)
-
-        @pl.when(jnp.logical_and(d > 0, (s + d) % n_rows != r))
-        def _():
-            greet(s, 2 * ((s + d) % n_rows) + k)
-
-        @pl.when(jnp.logical_not(diagonal))
-        def _():
-            greet((r + d) % n_rows, 2 * r + k)
+    def greet_reducers(t, _):
+        row = place(t)
+
+        @pl.when(jnp.logical_not(jnp.logical_and(row == r, in_line)))
+        def _():
+            greet(row, 2 * seat(s, row) + k)
+
+        @pl.when(jnp.logical_not(jnp.logical_and(row == r, in_plane)))
+        def _():
+            greet(row, 2 * seat(r, row) + k)
 
         return 0
 
-    lax.fori_loop(0, n_rows, greet_all, 0)
+    lax.fori_loop(0, SHARDS, greet_reducers, 0)
+
+    @pl.when(reducer)
+    def _():
+        def greet_members(d, _):
+            @pl.when(jnp.logical_not(jnp.logical_and(d == r, in_line)))
+            def _():
+                greet(d, 2 * hub + k)
+
+            @pl.when(jnp.logical_not(jnp.logical_and(d == s, in_plane)))
+            def _():
+                greet(hub, 2 * d + k)
+
+            return 0
+
+        lax.fori_loop(0, n_rows, greet_members, 0)
+
+    @pl.when(jnp.logical_not(diagonal))
+    def _():
+        greet(s, 2 * r + k)
+
+    greeted = (
+        1
+        + jnp.where(diagonal, 0, 1)
+        + 2 * SHARDS
+        + jnp.where(reducer, 2 * n_rows, 0)
+        - jnp.where(in_line, 2, 0)
+        - jnp.where(in_plane, 2, 0)
+    )
 
     def send(src, dst, send_sem, recv_sem, row, col):
         pltpu.make_async_remote_copy(
@@ -118,6 +164,17 @@
 
     def take(ref, sem):
         pltpu.make_async_copy(ref, ref, sem).wait()
+
+    def spread(src, dst, send_sem, recv_sem, d):
+        mine = jnp.logical_and(d == r, in_line)
+
+        @pl.when(mine)
+        def _():
+            pltpu.make_async_copy(src, dst, recv_sem).start()
+
+        @pl.when(jnp.logical_not(mine))
+        def _():
+            send(src, dst, send_sem, recv_sem, d, 2 * hub + k)
 
     def unfold(packed, lefts):
         def group(i, _):
@@ -176,15 +233,28 @@
     terms[:, :, 256:384] = jnp.zeros((slots, 64, 128), F32)
     unfold(first_ref, left_own)
 
+    pl.semaphore_wait(barrier, greeted)
+
     @pl.when(jnp.logical_not(diagonal))
     def _():
-        pl.semaphore_wait(barrier, 3 * n_rows - 2)
         send(first_ref, across.at[0, k], send_first, across_sem.at[0], s, 2 * r + k)
 
     @pl.when(diagonal)
     def _():
-        pl.semaphore_wait(barrier, 2 * n_rows - 1)
         pltpu.make_async_copy(first_ref, across.at[0, k], across_sem.at[0]).start()
+
+    @pl.when(reducer)
+    def _():
+        give[0] = back_ref[shard]
+        give[1] = scale_ref[shard % 3]
+
+        @pl.when(in_line)
+        def _():
+            pltpu.make_async_copy(give, given, given_sem).start()
+
+        @pl.when(jnp.logical_not(in_line))
+        def _():
+            send(give, given, send_given, given_sem, r, 2 * seat(s, r) + k)
 
     loads.wait()
 
@@ -194,29 +264,28 @@
         send(half.at[step, 1], half_in.at[step], send_half.at[step], half_sem.at[step], *other)
         gather_terms(row_pick, k, 2, half.at[step, 0])
 
+        take(half_in.at[step], half_sem.at[step])
+
+        def send_one(t, _):
+            direct[step, t] = (half[step, 0, t] + half_in[step, t]).astype(BF16)
+            row = place(t)
+            mine = jnp.logical_and(row == r, in_plane)
+            dst = arrived.at[step, s]
+
+            @pl.when(mine)
+            def _():
+                pltpu.make_async_copy(direct.at[step, t], dst, arrived_sem.at[step]).start()
+
+            @pl.when(jnp.logical_not(mine))
+            def _():
+                send(direct.at[step, t], dst, send_direct.at[step], arrived_sem.at[step], row, 2 * seat(r, row) + k)
+
+            return 0
+
+        lax.fori_loop(0, SHARDS, send_one, 0)
+
         take(across.at[step, k], across_sem.at[step])
         send(across.at[step, k], across.at[step, k], send_swap.at[step], swap_sem.at[step], *other)
-
-        take(half_in.at[step], half_sem.at[step])
-
-        def send_one(t, _):
-            direct[step, t] = (half[step, 0, t] + half_in[step, t]).astype(BF16)
-            row = (r + t) % n_rows
-            mine = jnp.logical_and(diagonal, t == 0)
-            dst = arrived.at[step, s]
-
-            @pl.when(mine)
-            def _():
-                pltpu.make_async_copy(direct.at[step, t], dst, arrived_sem.at[step]).start()
-
-            @pl.when(jnp.logical_not(mine))
-            def _():
-                send(direct.at[step, t], dst, send_direct.at[step], arrived_sem.at[step], row, 2 * r + k)
-
-            return 0
-
-        lax.fori_loop(0, SHARDS, send_one, 0)
-
         unfold(across.at[step, k], left_across.at[k])
         take(across.at[step, 1 - k], swap_sem.at[step])
         unfold(across.at[step, 1 - k], left_across.at[1 - k])
@@ -224,8 +293,8 @@
         gather_terms(col_pick, 0, 1, mirror.at[step])
 
         def send_mine(t, _):
-            row = (s + t) % n_rows
-            mine = row == r
+            row = place(t)
+            mine = jnp.logical_and(row == r, in_line)
             dst = arrived.at[step, n_rows + r]
 
             @pl.when(mine)
@@ -234,7 +303,7 @@
 
             @pl.when(jnp.logical_not(mine))
             def _():
-                send(mirror.at[step, t], dst, send_mirror.at[step], arrived_sem.at[step], row, c)
+                send(mirror.at[step, t], dst, send_mirror.at[step], arrived_sem.at[step], row, 2 * seat(s, row) + k)
 
             return 0
 
@@ -247,12 +316,17 @@
             def add(j, total):
                 return total + arrived[step, j].astype(F32)
 
-            field = lax.fori_loop(0, 2 * n_rows, add, back_ref[shard], unroll=4)
+
+            @pl.when(step == 0)
+            def _():
+                take(given, given_sem)
+
+            field = lax.fori_loop(0, 2 * n_rows, add, given[0], unroll=4)
             if final:
-                out_ref[shard] = field
+                last[...] = field
             else:
                 re, im = field[:8], field[8:]
-                scale_re, scale_im = scale_ref[0, shard % 3], scale_ref[1, shard % 3]
+                scale_re, scale_im = given[1, :8], given[1, 8:]
                 now[step, :8] = (scale_re * re - scale_im * im).astype(BF16)
                 now[step, 8:] = (scale_re * im + scale_im * re).astype(BF16)
 
@@ -264,24 +338,27 @@
             src = now.at[step]
             line = own.at[step, shard]
             plane = across.at[step + 1, k, shard]
-            pltpu.make_async_copy(src, line, own_sem.at[step]).start()
-
-            def spread(d, _):
-                @pl.when(jnp.logical_or(d > 0, r != s))
-                def _():
-                    send(src, plane, send_now.at[step], across_sem.at[step + 1], s, 2 * ((s + d) % n_rows) + k)
-
-                @pl.when(jnp.logical_and(d == 0, r == s))
+
+            def spread_line(d, _):
+                spread(src, line, send_now.at[step], own_sem.at[step], d)
+                return 0
+
+            lax.fori_loop(0, n_rows, spread_line, 0)
+
+            def spread_plane(d, _):
+                mine = jnp.logical_and(d == s, in_plane)
+
+                @pl.when(mine)
                 def _():
                     pltpu.make_async_copy(src, plane, across_sem.at[step + 1]).start()
 
-                @pl.when(d > 0)
+                @pl.when(jnp.logical_not(mine))
                 def _():
-                    send(src, line, send_now.at[step], own_sem.at[step], (r + d) % n_rows, c)
+                    send(src, plane, send_now.at[step], across_sem.at[step + 1], hub, 2 * d + k)
 
                 return 0
 
-            lax.fori_loop(0, n_rows, spread, 0)
+            lax.fori_loop(0, n_rows, spread_plane, 0)
 
         take(own.at[step], own_sem.at[step])
         unfold(own.at[step], left_own)
@@ -307,18 +384,22 @@
 
     @pl.when(reducer)
     def _():
-        def spread(d, _):
-            send(out_ref.at[shard], out_ref.at[shard], send_now.at[PRODUCTS - 1], out_sem, (r + d) % n_rows, c)
-            return 0
-
-        lax.fori_loop(1, n_rows, spread, 0)
-        take(out_ref.at[pl.ds(0, SHARDS - 1)], out_sem)
-        take(half.at[0, 0], send_now.at[PRODUCTS - 1])
-        take(half.at[0, 0, pl.ds(0, n_rows - 1 - SHARDS)], send_now.at[PRODUCTS - 1])
-
-    @pl.when(jnp.logical_not(reducer))
-    def _():
-        take(out_ref, out_sem)
+        def spread_last(d, _):
+            spread(last, out_ref.at[shard], send_now.at[PRODUCTS - 1], out_sem, d)
+            return 0
+
+        lax.fori_loop(0, n_rows, spread_last, 0)
+
+    take(out_ref, out_sem)
+
+    @pl.when(in_line)
+    def _():
+        take(arrived.at[0, pl.ds(0, 2 * n_rows - 2)], send_now.at[PRODUCTS - 1])
+
+    @pl.when(jnp.logical_and(reducer, hub != s))
+    def _():
+        take(arrived.at[0], send_now.at[PRODUCTS - 1])
+        take(given, send_given)
 
     @pl.when(jnp.logical_not(diagonal))
     def _():
@@ -328,31 +409,34 @@
         take(across.at[step, 0], send_swap.at[step])
         take(half_in.at[step], send_half.at[step])
 
-        @pl.when(diagonal)
-        def _():
-            take(direct.at[step, pl.ds(0, SHARDS - 1)], send_direct.at[step])
-
-        @pl.when(jnp.logical_not(diagonal))
-        def _():
-            take(direct.at[step], send_direct.at[step])
-
-        @pl.when(reducer)
-        def _():
-            take(mirror.at[step, pl.ds(0, SHARDS - 1)], send_mirror.at[step])
-
-            @pl.when(step < PRODUCTS - 1)
-            def _():
-                @pl.when(diagonal)
-                def _():
-                    take(arrived.at[step, pl.ds(0, 2 * n_rows - 2)], send_now.at[step])
-
-                @pl.when(jnp.logical_not(diagonal))
-                def _():
-                    take(arrived.at[step, pl.ds(0, 2 * n_rows - 1)], send_now.at[step])
-
-        @pl.when(jnp.logical_not(reducer))
-        def _():
-            take(mirror.at[step], send_mirror.at[step])
+        def sent(ref, less, send_sem):
+            @pl.when(less)
+            def _():
+                take(ref.at[pl.ds(0, SHARDS - 1)], send_sem)
+
+            @pl.when(jnp.logical_not(less))
+            def _():
+                take(ref, send_sem)
+
+        sent(direct.at[step], in_plane, send_direct.at[step])
+        sent(mirror.at[step], in_line, send_mirror.at[step])
+
+        @pl.when(jnp.logical_and(reducer, step < PRODUCTS - 1))
+        def _():
+            both = jnp.logical_and(in_line, in_plane)
+            either = jnp.logical_or(in_line, in_plane)
+
+            @pl.when(both)
+            def _():
+                take(arrived.at[step, pl.ds(0, 2 * n_rows - 2)], send_now.at[step])
+
+            @pl.when(jnp.logical_and(either, jnp.logical_not(both)))
+            def _():
+                take(arrived.at[step, pl.ds(0, 2 * n_rows - 1)], send_now.at[step])
+
+            @pl.when(jnp.logical_not(either))
+            def _():
+                take(arrived.at[step], send_now.at[step])
 
         return 0
 
@@ -382,14 +466,15 @@
     scale = jnp.tile(scale, (1, 1, 3))
     lanes = jnp.concatenate(
         [scale[..., :256].reshape(2, 1024), scale[..., 256:].reshape(2, 128)], axis=-1
-    ).reshape(2, 3, 1, 384)
-    scale = jnp.broadcast_to(lanes, (2, 3, 8, 384))
+    ).reshape(2, 3, 384)
+    scale = jnp.broadcast_to(lanes.transpose(1, 0, 2)[:, :, None], (3, 2, 8, 384)).reshape(3, 16, 384)
+    scale_re, scale_im = lanes[0, :, None], lanes[1, :, None]
 
     back = pack(background[:, :, :, 0, :])
     pairs = back.reshape(GROUPS, 3, 2, 8, 384)
     re, im = pairs[:, :, 0], pairs[:, :, 1]
     first = (
-        jnp.stack([scale[0] * re - scale[1] * im, scale[0] * im + scale[1] * re], axis=2)
+        jnp.stack([scale_re * re - scale_im * im, scale_re * im + scale_im * re], axis=2)
         .astype(BF16)
         .reshape(SHARDS, 16, 384)
     )
@@ -402,7 +487,7 @@
     field = pl.pallas_call(
         functools.partial(kernel, n_rows),
         out_shape=jax.ShapeDtypeStruct(packed, F32),
-        in_specs=[smem] * 4 + [pl.BlockSpec(memory_space=pl.ANY)] + [vmem] * 3,
+        in_specs=[smem] * 4 + [pl.BlockSpec(memory_space=pltpu.HBM)] + [vmem] * 3,
         out_specs=vmem,
         scratch_shapes=[
             pltpu.VMEM(green_blocks.shape[2:], BF16),
@@ -417,6 +502,9 @@
             pltpu.VMEM(steps + packed, BF16),
             pltpu.VMEM((PRODUCTS, 2 * n_rows, 16, 384), BF16),
             pltpu.VMEM((PRODUCTS, 16, 384), BF16),
+            pltpu.VMEM((16, 384), F32),
+            pltpu.VMEM((2, 16, 384), F32),
+            pltpu.VMEM((2, 16, 384), F32),
             dma(()),
             dma((PRODUCTS - 1,)),
             dma(steps),
@@ -430,9 +518,11 @@
             dma(steps),
             dma(steps),
             dma(steps),
+            dma(()),
+            dma(()),
         ],
         compiler_params=pltpu.CompilerParams(
-            collective_id=0, has_side_effects=True, vmem_limit_bytes=48 * 2**20
+            collective_id=0, has_side_effects=True, vmem_limit_bytes=60 * 2**20
         ),
     )(local_rows, local_cols, row_pick, col_pick, green_blocks, first, back, scale)
     return unpack(field)[:, :, :, None, :]

time: 137 us -> 125 us (0.912); the launches traced: 137 us -> 123 us
  Pallas kernels: 128 us -> 112 us
    pallas_call x1, Pallas kernels: 128 us -> 112 us  [local(): pl.pallas_call(functools.partial(kernel, n_rows), out_shape=jax.ShapeDtyp...]
    unnamed x10 -> x8, local copies, waits for them, and re-layouts: 2.54 us -> 0.04 us
where the time goes in v2:
time: 125 us; the launch traced here: 123 us
  Pallas kernels  112 us (90%)
  local copies, waits for them, and re-layouts  7.83 us (6%)
  other arithmetic  1.67 us (1%)
    pallas_call x1, Pallas kernels, local(): pl.pallas_call(functools.partial(kernel, n_rows), out_shape=jax.ShapeDtyp...  112 us

profile of v2, /device:TPU:1, one launch (start us, length us, event | category | flops | bytes accessed | tf_op | source)
XLA Modules:
  0.0 122.8 jit_solution(3213361883132341945)
XLA Ops:
  0.0 0.0 copy-start
  0.0 0.0 copy-start.1
  0.0 0.8 slice_bitcast_fusion.2
  0.8 0.8 select_reduce_fusion.1
  1.6 0.1 tile.10
  1.7 0.1 reshape.142
  1.8 1.0 copy_bitcast_fusion.2
  2.9 0.1 copy.27
  3.0 0.1 reshape.145
  3.1 0.1 reshape.146
  3.3 0.1 fusion.5
  3.4 0.7 pad_maximum_fusion.1
  4.1 0.6 broadcast_bitcast_fusion.scale_ref
  5.4 0.0 copy-done
  5.4 0.0 copy-done.1
  5.5 0.7 select_n.44.row_pick
  6.2 0.6 select_n.48.col_pick
  6.7 0.7 copy.30
  7.5 112.5 %shard_map.73 = f32[12,16,384]{2,1,0:T(8,128)} custom-call(s32[12]{0:T(128)} %bitcast.55, s32[12]{0:T(128)} %bitcast.57, f32[96]{0:T(128)} %select_n.44.row_pick, f32[48]{0:T(128)} %select_n.48.col_pick, bf16[1,1,12,2,288,288]{5,4,3,2,1,0:T(8,128)(2,1)} %g_hbm.1, bf16[12,16,384]{2,1,0:T(8,128)(2,1)} %bitcast.50, f32[12,16,384]{2,1,0:T(8,128)} %bitcast.47, ...), custom_call_target="tpu_custom_call" | custom-call | tf_op jit(solution)/shard_map/pallas_call | solution.py:487
  119.9 1.1 copy.49
  121.1 0.2 reshape.151
  121.3 0.1 concatenate.16
  121.4 0.1 concatenate.17
  121.5 0.1 maximum_bitcast_fusion
  121.7 1.2 copy.34
  (23 shorter events, 0.3 us)
Async XLA Ops:
  0.0 5.4 %copy-start = (s32[1,1,12]{2,1,0:T(1,128)S(1)}, s32[1,1,12]{2,1,0:T(1,128)}, u32[]{:S(2)}) copy-start(s32[1,1,12]{2,1,0:T(1,128)} %param.8) | copy-start | bytes 148
  0.0 5.4 %copy-start.1 = (s32[1,1,12]{2,1,0:T(1,128)S(1)}, s32[1,1,12]{2,1,0:T(1,128)}, u32[]{:S(2)}) copy-start(s32[1,1,12]{2,1,0:T(1,128)} %param.9) | copy-start | bytes 148

commit v3 on v2

--- a/solution.py
+++ b/solution.py
@@ -194,7 +194,7 @@
                 put(q, 256, pltpu.roll(tail, 128 - 32 * q, 1))
             return 0
 
-        lax.fori_loop(0, GROUPS, group, 0)
+        lax.fori_loop(0, GROUPS, group, 0, unroll=True)
 
     def products(lefts, picks, dims):
         def one(slot, _):
@@ -206,7 +206,7 @@
             ) + lax.dot_general(im, g[slot, 1], dims, preferred_element_type=F32)
             return 0
 
-        lax.fori_loop(0, slots, one, 0)
+        lax.fori_loop(0, slots, one, 0, unroll=4)
 
     def gather_terms(pick, first, step, out):
         def group(i, _):
@@ -228,7 +228,7 @@
             out[3 * i + 2, :, 256:384] = tail.astype(out.dtype)
             return 0
 
-        lax.fori_loop(0, GROUPS, group, 0)
+        lax.fori_loop(0, GROUPS, group, 0, unroll=True)
 
     terms[:, :, 256:384] = jnp.zeros((slots, 64, 128), F32)
     unfold(first_ref, left_own)
@@ -321,7 +321,7 @@
             def _():
                 take(given, given_sem)
 
-            field = lax.fori_loop(0, 2 * n_rows, add, given[0], unroll=4)
+            field = lax.fori_loop(0, 2 * n_rows, add, given[0], unroll=8)
             if final:
                 last[...] = field
             else:
@@ -373,7 +373,7 @@
             ) + lax.dot_general(im, g[slot, 1], NN, preferred_element_type=F32)
             return 0
 
-        lax.fori_loop(0, slots, one, 0)
+        lax.fori_loop(0, slots, one, 0, unroll=4)
 
     def early(step, _):
         update(step, False)

time: 125 us -> 120 us (0.960); the launches traced: 123 us -> 119 us
  Pallas kernels: 112 us -> 109 us
    pallas_call x1, Pallas kernels: 112 us -> 109 us  [local(): pl.pallas_call(functools.partial(kernel, n_rows), out_shape=jax.ShapeDtyp...]
where the time goes in v3:
time: 120 us; the launch traced here: 119 us
  Pallas kernels  109 us (91%)
  local copies, waits for them, and re-layouts  7.83 us (7%)
  other arithmetic  1.67 us (1%)
    pallas_call x1, Pallas kernels, local(): pl.pallas_call(functools.partial(kernel, n_rows), out_shape=jax.ShapeDtyp...  109 us

profile of v3, /device:TPU:1, one launch (start us, length us, event | category | flops | bytes accessed | tf_op | source)
XLA Modules:
  0.0 119.3 jit_solution(9865908263469847563)
XLA Ops:
  0.0 0.0 copy-start
  0.0 0.0 copy-start.1
  0.0 0.8 slice_bitcast_fusion.2
  0.8 0.8 select_reduce_fusion.1
  1.6 0.1 tile.10
  1.7 0.1 reshape.142
  1.8 1.0 copy_bitcast_fusion.2
  2.9 0.1 copy.27
  3.0 0.1 reshape.145
  3.1 0.1 reshape.146
  3.3 0.1 fusion.5
  3.4 0.7 pad_maximum_fusion.1
  4.1 0.6 broadcast_bitcast_fusion.scale_ref
  5.4 0.0 copy-done
  5.4 0.0 copy-done.1
  5.5 0.7 select_n.44.row_pick
  6.2 0.6 select_n.48.col_pick
  6.7 0.7 copy.30
  7.5 109.0 %shard_map.73 = f32[12,16,384]{2,1,0:T(8,128)} custom-call(s32[12]{0:T(128)} %bitcast.55, s32[12]{0:T(128)} %bitcast.57, f32[96]{0:T(128)} %select_n.44.row_pick, f32[48]{0:T(128)} %select_n.48.col_pick, bf16[1,1,12,2,288,288]{5,4,3,2,1,0:T(8,128)(2,1)} %g_hbm.1, bf16[12,16,384]{2,1,0:T(8,128)(2,1)} %bitcast.50, f32[12,16,384]{2,1,0:T(8,128)} %bitcast.47, ...), custom_call_target="tpu_custom_call" | custom-call | tf_op jit(solution)/shard_map/pallas_call | solution.py:487
  116.5 1.1 copy.49
  117.6 0.2 reshape.151
  117.8 0.1 concatenate.16
  117.9 0.1 concatenate.17
  118.1 0.1 maximum_bitcast_fusion
  118.2 1.2 copy.34
  (23 shorter events, 0.3 us)
Async XLA Ops:
  0.0 5.4 %copy-start = (s32[1,1,12]{2,1,0:T(1,128)S(1)}, s32[1,1,12]{2,1,0:T(1,128)}, u32[]{:S(2)}) copy-start(s32[1,1,12]{2,1,0:T(1,128)} %param.8) | copy-start | bytes 148
  0.0 5.4 %copy-start.1 = (s32[1,1,12]{2,1,0:T(1,128)S(1)}, s32[1,1,12]{2,1,0:T(1,128)}, u32[]{:S(2)}) copy-start(s32[1,1,12]{2,1,0:T(1,128)} %param.9) | copy-start | bytes 148

commit v4 on v3

--- a/solution.py
+++ b/solution.py
@@ -206,9 +206,9 @@
             ) + lax.dot_general(im, g[slot, 1], dims, preferred_element_type=F32)
             return 0
 
-        lax.fori_loop(0, slots, one, 0, unroll=4)
-
-    def gather_terms(pick, first, step, out):
+        lax.fori_loop(0, slots, one, 0, unroll=slots)
+
+    def gather_terms(pick, first, step, out, after=None):
         def group(i, _):
             at = pl.ds(pl.multiple_of(16 * i, 16), 16)
             tail = None
@@ -226,6 +226,8 @@
                 last = pltpu.roll(last, 32 * q, 1) if q else last
                 tail = last if tail is None else tail + last
             out[3 * i + 2, :, 256:384] = tail.astype(out.dtype)
+            if after is not None:
+                after(i)
             return 0
 
         lax.fori_loop(0, GROUPS, group, 0, unroll=True)
@@ -260,8 +262,11 @@
 
     def update(step, final):
         products(left_own, cols_ref, NT)
-        gather_terms(row_pick, 1 - k, 2, half.at[step, 1])
-        send(half.at[step, 1], half_in.at[step], send_half.at[step], half_sem.at[step], *other)
+        def send_half_group(i):
+            part = pl.ds(3 * i, 3)
+            send(half.at[step, 1, part], half_in.at[step, part], send_half.at[step], half_sem.at[step], *other)
+
+        gather_terms(row_pick, 1 - k, 2, half.at[step, 1], send_half_group)
         gather_terms(row_pick, k, 2, half.at[step, 0])
 
         take(half_in.at[step], half_sem.at[step])
@@ -290,8 +295,6 @@
         take(across.at[step, 1 - k], swap_sem.at[step])
         unfold(across.at[step, 1 - k], left_across.at[1 - k])
         products_across()
-        gather_terms(col_pick, 0, 1, mirror.at[step])
-
         def send_mine(t, _):
             row = place(t)
             mine = jnp.logical_and(row == r, in_line)
@@ -307,7 +310,11 @@
 
             return 0
 
-        lax.fori_loop(0, SHARDS, send_mine, 0)
+        def send_mine_group(i):
+            for part in range(3):
+                send_mine(3 * i + part, 0)
+
+        gather_terms(col_pick, 0, 1, mirror.at[step], send_mine_group)
 
         @pl.when(reducer)
         def _():
@@ -373,7 +380,7 @@
             ) + lax.dot_general(im, g[slot, 1], NN, preferred_element_type=F32)
             return 0
 
-        lax.fori_loop(0, slots, one, 0, unroll=4)
+        lax.fori_loop(0, slots, one, 0, unroll=slots)
 
     def early(step, _):
         update(step, False)
@@ -522,7 +529,7 @@
             dma(()),
         ],
         compiler_params=pltpu.CompilerParams(
-            collective_id=0, has_side_effects=True, vmem_limit_bytes=60 * 2**20
+            collective_id=0, has_side_effects=True, vmem_limit_bytes=32 * 2**20
         ),
     )(local_rows, local_cols, row_pick, col_pick, green_blocks, first, back, scale)
     return unpack(field)[:, :, :, None, :]

time: 120 us -> 115 us (0.958)
  Pallas kernels: 109 us -> 105 us
    pallas_call x1, Pallas kernels: 109 us -> 105 us  [local(): pl.pallas_call(functools.partial(kernel, n_rows), out_shape=jax.ShapeDtyp...]
    unnamed x8 -> x10, local copies, waits for them, and re-layouts: 0.04 us -> 2.54 us
where the time goes in v4:
time: 115 us; the launch traced here: 114 us
  Pallas kernels  105 us (91%)
  local copies, waits for them, and re-layouts  6.92 us (6%)
    pallas_call x1, Pallas kernels, local(): pl.pallas_call(functools.partial(kernel, n_rows), out_shape=jax.ShapeDtyp...  105 us
    unnamed x10, local copies, waits for them, and re-layouts  2.54 us

profile of v4, /device:TPU:1, one launch (start us, length us, event | category | flops | bytes accessed | tf_op | source)
XLA Modules:
  0.0 113.7 jit_solution(4781962277076811958)
XLA Ops:
  0.0 0.0 copy-start.1
  0.0 0.0 copy-start.2
  0.0 0.8 slice_bitcast_fusion.2
  0.8 0.8 select_reduce_fusion.1
  1.6 0.1 tile.10
  1.7 0.1 reshape.142
  1.8 1.0 copy_bitcast_fusion.2
  2.9 0.1 copy.27
  3.0 0.1 reshape.145
  3.1 0.1 reshape.146
  3.3 0.1 fusion.5
  4.1 0.0 copy-done.1
  4.1 0.0 copy-done.2
  4.2 0.1 select_n.44.row_pick
  4.3 0.1 select_n.48.col_pick
  4.4 0.0 copy-start
  4.4 2.5 %copy-done = bf16[1,1,12,2,288,288]{5,4,3,2,1,0:T(8,128)(2,1)S(1)} copy-done((bf16[1,1,12,2,288,288]{5,4,3,2,1,0:T(8,128)(2,1)S(1)}, bf16[1,1,12,2,288,288]{5,4,3,2,1,0:T(8,128)(2,1)}, u32[]{:S(2)}) %copy-start) | copy-done | bytes 3981336
  6.9 104.9 %shard_map.73 = f32[12,16,384]{2,1,0:T(8,128)S(1)} custom-call(s32[12]{0:T(128)S(1)} %bitcast.47, s32[12]{0:T(128)S(1)} %bitcast.49, f32[96]{0:T(128)S(1)} %select_n.44.row_pick, f32[48]{0:T(128)S(1)} %select_n.48.col_pick, bf16[1,1,12,2,288,288]{5,4,3,2,1,0:T(8,128)(2,1)S(1)} %copy-done, bf16[12,16,384]{2,1,0:T(8,128)(2,1)S(1)} %bitcast.45, ...), custom_call_target="tpu_custom_call" | custom-call | tf_op jit(solution)/shard_map/pallas_call | solution.py:494
  111.8 0.2 copy.49
  111.9 0.2 reshape.151
  112.1 0.1 concatenate.16
  112.3 0.1 concatenate.17
  112.4 0.1 maximum_bitcast_fusion
  112.5 1.2 %copy.34 = f32[2,32,4,1,288]{4,3,2,1,0:T(1,128)} copy(f32[2,32,4,1,288]{4,1,2,0,3:T(8,128)S(1)} %bitcast.52) | data formatting | bytes 589824 | tf_op jit(solution)/shard_map/broadcast_in_dim;reshape | solution.py:535
  (26 shorter events, 0.4 us)
Async XLA Ops:
  0.0 4.1 %copy-start.1 = (s32[1,1,12]{2,1,0:T(1,128)S(1)}, s32[1,1,12]{2,1,0:T(1,128)}, u32[]{:S(2)}) copy-start(s32[1,1,12]{2,1,0:T(1,128)} %param.8) | copy-start | bytes 148
  0.0 4.1 %copy-start.2 = (s32[1,1,12]{2,1,0:T(1,128)S(1)}, s32[1,1,12]{2,1,0:T(1,128)}, u32[]{:S(2)}) copy-start(s32[1,1,12]{2,1,0:T(1,128)} %param.9) | copy-start | bytes 148
  4.4 2.5 %copy-start = (bf16[1,1,12,2,288,288]{5,4,3,2,1,0:T(8,128)(2,1)S(1)}, bf16[1,1,12,2,288,288]{5,4,3,2,1,0:T(8,128)(2,1)}, u32[]{:S(2)}) copy-start(bf16[1,1,12,2,288,288]{5,4,3,2,1,0:T(8,128)(2,1)} %g_hbm.1) | copy-start | bytes 11943940

commit v5 on v4

--- a/solution.py
+++ b/solution.py
@@ -208,8 +208,9 @@
 
         lax.fori_loop(0, slots, one, 0, unroll=slots)
 
-    def gather_terms(pick, first, step, out, after=None):
+    def gather_terms(pick, first, step, out, after=None, start=None):
         def group(i, _):
+            i = i if start is None else (i + start) % GROUPS
             at = pl.ds(pl.multiple_of(16 * i, 16), 16)
             tail = None
             for q in range(4):
@@ -262,6 +263,7 @@
 
     def update(step, final):
         products(left_own, cols_ref, NT)
+
         def send_half_group(i):
             part = pl.ds(3 * i, 3)
             send(half.at[step, 1, part], half_in.at[step, part], send_half.at[step], half_sem.at[step], *other)
@@ -272,6 +274,7 @@
         take(half_in.at[step], half_sem.at[step])
 
         def send_one(t, _):
+            t = (t + s) % SHARDS
             direct[step, t] = (half[step, 0, t] + half_in[step, t]).astype(BF16)
             row = place(t)
             mine = jnp.logical_and(row == r, in_plane)
@@ -295,6 +298,7 @@
         take(across.at[step, 1 - k], swap_sem.at[step])
         unfold(across.at[step, 1 - k], left_across.at[1 - k])
         products_across()
+
         def send_mine(t, _):
             row = place(t)
             mine = jnp.logical_and(row == r, in_line)
@@ -314,7 +318,7 @@
             for part in range(3):
                 send_mine(3 * i + part, 0)
 
-        gather_terms(col_pick, 0, 1, mirror.at[step], send_mine_group)
+        gather_terms(col_pick, 0, 1, mirror.at[step], send_mine_group, r)
 
         @pl.when(reducer)
         def _():
@@ -347,13 +351,14 @@
             plane = across.at[step + 1, k, shard]
 
             def spread_line(d, _):
-                spread(src, line, send_now.at[step], own_sem.at[step], d)
+                spread(src, line, send_now.at[step], own_sem.at[step], (r + d) % n_rows)
                 return 0
 
             lax.fori_loop(0, n_rows, spread_line, 0)
 
             def spread_plane(d, _):
-                mine = jnp.logical_and(d == s, in_plane)
+                seat_d = (s + d) % n_rows
+                mine = jnp.logical_and(seat_d == s, in_plane)
 
                 @pl.when(mine)
                 def _():
@@ -361,7 +366,7 @@
 
                 @pl.when(jnp.logical_not(mine))
                 def _():
-                    send(src, plane, send_now.at[step], across_sem.at[step + 1], hub, 2 * d + k)
+                    send(src, plane, send_now.at[step], across_sem.at[step + 1], hub, 2 * seat_d + k)
 
                 return 0
 
@@ -392,7 +397,7 @@
     @pl.when(reducer)
     def _():
         def spread_last(d, _):
-            spread(last, out_ref.at[shard], send_now.at[PRODUCTS - 1], out_sem, d)
+            spread(last, out_ref.at[shard], send_now.at[PRODUCTS - 1], out_sem, (r + d) % n_rows)
             return 0
 
         lax.fori_loop(0, n_rows, spread_last, 0)

time: 115 us -> 117 us (1.017); the launches traced: 114 us -> 117 us
  Pallas kernels: 105 us -> 108 us
    pallas_call x1, Pallas kernels: 105 us -> 108 us  [local(): pl.pallas_call(functools.partial(kernel, n_rows), out_shape=jax.ShapeDtyp...]
where the time goes in v5:
time: 117 us
  Pallas kernels  108 us (92%)
  local copies, waits for them, and re-layouts  6.92 us (6%)
    pallas_call x1, Pallas kernels, local(): pl.pallas_call(functools.partial(kernel, n_rows), out_shape=jax.ShapeDtyp...  108 us
    unnamed x10, local copies, waits for them, and re-layouts  2.54 us

profile of v5, /device:TPU:1, one launch (start us, length us, event | category | flops | bytes accessed | tf_op | source)
XLA Modules:
  0.0 117.2 jit_solution(15345248852502357988)
XLA Ops:
  0.0 0.0 copy-start.1
  0.0 0.0 copy-start.2
  0.0 0.8 slice_bitcast_fusion.2
  0.8 0.8 select_reduce_fusion.1
  1.6 0.1 tile.10
  1.7 0.1 reshape.142
  1.8 1.0 copy_bitcast_fusion.2
  2.9 0.1 copy.27
  3.0 0.1 reshape.145
  3.1 0.1 reshape.146
  3.3 0.1 fusion.5
  4.1 0.0 copy-done.1
  4.1 0.0 copy-done.2
  4.2 0.1 select_n.44.row_pick
  4.3 0.1 select_n.48.col_pick
  4.4 0.0 copy-start
  4.4 2.5 %copy-done = bf16[1,1,12,2,288,288]{5,4,3,2,1,0:T(8,128)(2,1)S(1)} copy-done((bf16[1,1,12,2,288,288]{5,4,3,2,1,0:T(8,128)(2,1)S(1)}, bf16[1,1,12,2,288,288]{5,4,3,2,1,0:T(8,128)(2,1)}, u32[]{:S(2)}) %copy-start) | copy-done | bytes 3981336
  6.9 108.4 %shard_map.73 = f32[12,16,384]{2,1,0:T(8,128)S(1)} custom-call(s32[12]{0:T(128)S(1)} %bitcast.47, s32[12]{0:T(128)S(1)} %bitcast.49, f32[96]{0:T(128)S(1)} %select_n.44.row_pick, f32[48]{0:T(128)S(1)} %select_n.48.col_pick, bf16[1,1,12,2,288,288]{5,4,3,2,1,0:T(8,128)(2,1)S(1)} %copy-done, bf16[12,16,384]{2,1,0:T(8,128)(2,1)S(1)} %bitcast.45, ...), custom_call_target="tpu_custom_call" | custom-call | tf_op jit(solution)/shard_map/pallas_call | solution.py:499
  115.3 0.2 copy.49
  115.5 0.2 reshape.151
  115.7 0.1 concatenate.16
  115.8 0.1 concatenate.17
  115.9 0.1 maximum_bitcast_fusion
  116.1 1.2 copy.34
  (26 shorter events, 0.4 us)
Async XLA Ops:
  0.0 4.1 %copy-start.1 = (s32[1,1,12]{2,1,0:T(1,128)S(1)}, s32[1,1,12]{2,1,0:T(1,128)}, u32[]{:S(2)}) copy-start(s32[1,1,12]{2,1,0:T(1,128)} %param.8) | copy-start | bytes 148
  0.0 4.1 %copy-start.2 = (s32[1,1,12]{2,1,0:T(1,128)S(1)}, s32[1,1,12]{2,1,0:T(1,128)}, u32[]{:S(2)}) copy-start(s32[1,1,12]{2,1,0:T(1,128)} %param.9) | copy-start | bytes 148
  4.4 2.5 %copy-start = (bf16[1,1,12,2,288,288]{5,4,3,2,1,0:T(8,128)(2,1)S(1)}, bf16[1,1,12,2,288,288]{5,4,3,2,1,0:T(8,128)(2,1)}, u32[]{:S(2)}) copy-start(bf16[1,1,12,2,288,288]{5,4,3,2,1,0:T(8,128)(2,1)} %g_hbm.1) | copy-start | bytes 11943940
